TPU v7x, 512 devices: a whole 4x4x16 slice. The times are simulated.
512 devices in a mesh: dp: 16 (over z), ctx: 32 (over x, y, core).
Axes of the slice: x: 4, y: 4, z: 16, core: 2. Of those that a mesh axis runs over, the one named last changes fastest.
Arguments:
- tokens: bfloat16 [16, 8192, 1024], P('dp', 'ctx'), may hold values from -14 to 14
- w_query: bfloat16 [1024, 1024], replicated, may hold values from -0.1875 to 0.1875
- key_weight: bfloat16 [1024, 256], replicated, may hold values from -0.1875 to 0.1875
- value_weight: bfloat16 [1024, 256], replicated, may hold values from -0.1875 to 0.1875
- cotangent: bfloat16 [16, 8192, 1024], P('dp', 'ctx'), may hold values from -6 to 6
- segment_ids: int32 [16, 8192], P('dp'), may hold values from 0 to 3, never falling along the last dimension, each value on 1 to 4096 neighbouring positions
Outputs:
- grad_inputs: bfloat16 [16, 8192, 1024], P('dp', 'ctx')
- grad_query: float32 [1024, 1024], P('ctx')
- key_weight_gradient: float32 [1024, 256], P('ctx')
- value_weight_gradient: float32 [1024, 256], P('ctx')
Inputs may be any that keep to these rules, and one draw needn't show every extreme that they name: `segment_ids`: along each sequence the document numbers never fall and start at 0; each document has 1 to min(4096, 6144) bytes, and one has exactly that many.
All inputs are finite; a program needn't handle non-finite values.
Results may differ from a plain program's by a relative error of at most 0.014.
The roundings to bfloat16 on the way count: a program that leaves them out, or rounds other values in their place, can miss the bound.
Values may be sent and summed in bfloat16 or wider, within the bound.
A program may use at most 64 MiB of HBM per device.

v0:
```python
import jax
import jax.numpy as jnp
from jax import lax
from jax.sharding import PartitionSpec as P

HEAD_DIMENSION = 128
WINDOW = 1024
NEG_FILL = -1e30


def shifted(block, axis, distance):
    devices = range(lax.axis_size(axis))
    route = [(i - distance, i) for i in devices if i - distance in devices]
    return lax.ppermute(block, axis, route)


def head_terms(
    head_index, q_block, k_block, v_block, c_block, allowed, scale, head_size, group_size
):
    query_group = head_index // group_size
    query = lax.dynamic_slice_in_dim(q_block, head_index * head_size, head_size, 1)
    key_h = lax.dynamic_slice_in_dim(k_block, query_group * head_size, head_size, 1)
    value_h = lax.dynamic_slice_in_dim(v_block, query_group * head_size, head_size, 1)
    dout = lax.dynamic_slice_in_dim(c_block, head_index * head_size, head_size, 1)
    scores = jnp.dot(query, key_h.T, preferred_element_type=jnp.float32) * scale
    scores = jnp.where(allowed, scores, NEG_FILL)
    peak = jnp.max(scores, axis=1, keepdims=True)
    weights = jnp.exp(scores - peak)
    weights = weights / jnp.sum(weights, axis=1, keepdims=True)
    weights_b = weights.astype(jnp.bfloat16)
    attended = jnp.dot(weights_b, value_h, preferred_element_type=jnp.float32)
    delta = jnp.sum(dout.astype(jnp.float32) * attended, axis=1, keepdims=True)
    dprobs = jnp.dot(dout, value_h.T, preferred_element_type=jnp.float32)
    dscores = (weights * (dprobs - delta) * scale).astype(jnp.bfloat16)
    grad_q = jnp.dot(dscores, key_h, preferred_element_type=jnp.float32)
    key_gradient = jnp.dot(dscores.T, query, preferred_element_type=jnp.float32)
    value_gradient = jnp.dot(weights_b.T, dout, preferred_element_type=jnp.float32)
    return (grad_q, key_gradient, value_gradient)


def body(tokens, w_query, key_weight, value_weight, cotangent, segment_ids):
    sequence = tokens[0]
    cot = cotangent[0]
    seg = segment_ids[0]
    rows = sequence.shape[0]
    q_cols = w_query.shape[1]
    key_value_columns = key_weight.shape[1]
    head_size = HEAD_DIMENSION
    heads = q_cols // head_size
    kv_heads = key_value_columns // head_size
    group_size = heads // kv_heads
    reach = WINDOW // rows
    column_width = (reach + 1) * rows
    scale = head_size ** (-0.5)
    position = lax.axis_index("ctx")
    start = position * rows
    queries = jnp.dot(sequence, w_query, preferred_element_type=jnp.float32).astype(jnp.bfloat16)
    keys = jnp.dot(sequence, key_weight, preferred_element_type=jnp.float32).astype(jnp.bfloat16)
    values = jnp.dot(sequence, value_weight, preferred_element_type=jnp.float32).astype(
        jnp.bfloat16
    )
    earlier = [shifted((keys, values), "ctx", reach - slot) for slot in range(reach)]
    k_block = jnp.concatenate([pair[0] for pair in earlier] + [keys], axis=0)
    v_block = jnp.concatenate([pair[1] for pair in earlier] + [values], axis=0)
    seg_pad = jnp.concatenate([-jnp.ones((WINDOW,), jnp.int32), seg], axis=0)
    q_seg = lax.dynamic_slice_in_dim(seg, start, rows, 0)
    k_seg = lax.dynamic_slice_in_dim(seg_pad, start, column_width, 0)
    q_pos = start + jnp.arange(rows, dtype=jnp.int32)
    k_pos = start - reach * rows + jnp.arange(column_width, dtype=jnp.int32)
    gap = q_pos[:, None] - k_pos[None, :]
    allowed = (
        (gap >= 0) & (gap < WINDOW) & (k_pos[None, :] >= 0) & (q_seg[:, None] == k_seg[None, :])
    )
    grad_q, key_gradient, value_gradient = lax.map(
        lambda head_index: head_terms(
            head_index, queries, k_block, v_block, cot, allowed, scale, head_size, group_size
        ),
        jnp.arange(heads, dtype=jnp.int32),
    )
    dq_local = grad_q.transpose(1, 0, 2).reshape(rows, q_cols).astype(jnp.bfloat16)
    dk_local = (
        key_gradient.reshape(kv_heads, group_size, column_width, head_size)
        .sum(axis=1)
        .transpose(1, 0, 2)
        .reshape(column_width, key_value_columns)
    )
    dv_local = (
        value_gradient.reshape(kv_heads, group_size, column_width, head_size)
        .sum(axis=1)
        .transpose(1, 0, 2)
        .reshape(column_width, key_value_columns)
    )

    def piece(distance):
        first = (reach - distance) * rows
        return (dk_local[first : first + rows], dv_local[first : first + rows])

    dk_total, dv_total = piece(0)
    for distance in range(1, reach + 1):
        got_k, got_v = shifted(piece(distance), "ctx", -distance)
        dk_total = dk_total + got_k
        dv_total = dv_total + got_v
    dk_b = dk_total.astype(jnp.bfloat16)
    dv_b = dv_total.astype(jnp.bfloat16)
    grad_in = (
        jnp.dot(dq_local, w_query.T, preferred_element_type=jnp.float32)
        + jnp.dot(dk_b, key_weight.T, preferred_element_type=jnp.float32)
        + jnp.dot(dv_b, value_weight.T, preferred_element_type=jnp.float32)
    ).astype(jnp.bfloat16)
    combined = jnp.concatenate([dq_local, dk_b, dv_b], axis=1)
    partial_value = lax.dot_general(
        sequence, combined, (((0,), (0,)), ((), ())), preferred_element_type=jnp.float32
    )
    summed = lax.psum_scatter(
        lax.optimization_barrier(partial_value.astype(jnp.bfloat16))
        .astype(jnp.float32)
        .astype(jnp.bfloat16),
        "ctx",
        scatter_dimension=0,
        tiled=True,
    ).astype(jnp.float32)
    summed = lax.psum(summed, "dp")
    norm_factor = (lax.axis_size("dp") * lax.axis_size("ctx") * rows) ** (-0.5)
    summed = summed * norm_factor
    grad_query = summed[:, :q_cols]
    key_weight_gradient = summed[:, q_cols : q_cols + key_value_columns]
    value_weight_gradient = summed[:, q_cols + key_value_columns :]
    return (grad_in[None], grad_query, key_weight_gradient, value_weight_gradient)


def solution(mesh):
    placed = (P("dp", "ctx", None), P(), P(), P(), P("dp", "ctx", None), P("dp", None))
    return jax.shard_map(
        body,
        mesh=mesh,
        in_specs=placed,
        out_specs=(P("dp", "ctx", None), P("ctx", None), P("ctx", None), P("ctx", None)),
        check_vma=False,
    )
```

profile of v0, /device:TPU:16, one launch (start us, length us, event | category | flops | bytes accessed | tf_op | source)
XLA Modules:
  0.0 430.2 jit_solution(338459970549987686)
XLA Ops:
  10.8 3.2 collective-permute-start.6
  14.0 4.1 collective-permute-start.5
  19.6 3.2 collective-permute-start.1
  22.8 3.2 collective-permute-start
  32.8 3.7 collective-permute-start.2
  37.4 2.7 collective-permute-start.3
  41.0 6.0 %collective-permute-start.4 = (bf16[256,256]{1,0:T(8,128)(2,1)S(1)}, bf16[256,256]{1,0:T(8,128)(2,1)S(1)}, u32[]{:S(2)}, u32[]{:S(2)}) collective-permute-start(bf16[256,256]{1,0:T(8,128)(2,1)S(1)} %convolution_convert_fusion.2), channel_id=1, source_target_pairs={{0,4},{1,5},{2,6},{3,7},{4,8},{5,9},{6,10},{7,11},{8,12},{9,13},{1... | collective-permute-start | bytes 393224 | tf_op jit(solution)/shard_map/ppermute | solution.py:14
  47.1 3.2 collective-permute-done.4
  54.0 116.8 %while.17 = (s32[]{:T(128)}, bf16[8,256,128]{1,2,0:T(8,128)(2,1)}, f32[8,1280,128]{2,1,0:T(8,128)}, f32[8,1280,128]{2,1,0:T(8,128)}, s32[8]{0:T(128)S(1)}, /*ind...) while((s32[]{:T(128)}, bf16[8,256,128]{1,2,0:T(8,128)(2,1)}, ...), condition=%wide.region_4.5_spmd.clone, body=%wide.region_0.4_spmd.clone.sunk | while | flops 511278368 | bytes 14253591 | solution.py:74
  64.3 2.2 fusion.103
  78.9 2.2 fusion.103
  122.6 2.3 fusion.103
  137.2 2.3 fusion.103
  166.4 2.2 fusion.103
  170.7 2.9 bitcast_reduce_fusion
  181.7 2.2 collective-permute-start.13
  187.8 2.9 bitcast_reduce_fusion.1
  205.9 7.3 %collective-permute-done.15 = f32[256,256]{0,1:T(8,128)} collective-permute-done((f32[256,256]{0,1:T(8,128)}, f32[256,256]{0,1:T(8,128)}, u32[]{:S(2)}, u32[]{:S(2)}) %collective-permute-start.15) | collective-permute-done | bytes 262176 | tf_op jit(solution)/shard_map/ppermute | solution.py:14
  214.4 2.3 collective-permute-done.9
  216.8 22.7 %collective-permute-done.11 = f32[256,256]{0,1:T(8,128)} collective-permute-done((f32[256,256]{0,1:T(8,128)}, f32[256,256]{0,1:T(8,128)}, u32[]{:S(2)}, u32[]{:S(2)}) %collective-permute-start.11) | collective-permute-done | bytes 262176 | tf_op jit(solution)/shard_map/ppermute | solution.py:14
  240.7 2.7 fusion.33
  243.4 4.7 %copy.39 = bf16[1024,1536]{1,0:T(8,128)(2,1)} copy(bf16[1024,1536]{0,1:T(8,128)(2,1)} %fusion.33) | data formatting | bytes 6291456
  252.3 101.2 %reduce-scatter.4.cloned.1.call-done = bf16[32,1536]{1,0:T(8,128)(2,1)} async-done(((bf16[1024,1536]{1,0:T(8,128)(2,1)}), bf16[32,1536]{1,0:T(8,128)(2,1)}) %reduce-scatter.4.cloned.1.call-update) | async-done | bytes 98320
  354.6 66.4 %all-reduce.2 = f32[32,1536]{0,1:T(8,128)S(1)} all-reduce(bf16[32,1536]{0,1:T(8,128)(2,1)S(1)} %copy.40), channel_id=1, replica_groups=mesh['dp'=16,'ctx'=32] {'dp'}, use_global_device_ids=true, to_apply=%region_8.9 | all-reduce | flops 49152 | bytes 294912 | tf_op jit(solution)/shard_map/psum | solution.py:122
  (167 shorter events, 133.9 us)
Async XLA Ops:
  7.2 19.4 %copy-start = (bf16[1024,1024]{1,0:T(8,128)(2,1)S(1)}, bf16[1024,1024]{1,0:T(8,128)(2,1)}, u32[]{:S(2)}) copy-start(bf16[1024,1024]{1,0:T(8,128)(2,1)} %param.9) | copy-start | bytes 6291460
  7.2 19.4 %copy-start.2 = (bf16[1,256,1024]{2,1,0:T(8,128)(2,1)S(1)}, bf16[1,256,1024]{2,1,0:T(8,128)(2,1)}, u32[]{:S(2)}) copy-start(bf16[1,256,1024]{2,1,0:T(8,128)(2,1)} %param.8) | copy-start | bytes 1572868
  7.2 346.3 %reduce-scatter.4.cloned.1.call-start = ((), (), s32[]{:S(2)}) async-start(), calls=%async_computation.1 | async-start | bytes 3244032
  8.9 43.3 %collective-permute-start.7 = (bf16[256,256]{1,0:T(8,128)(2,1)S(1)}, bf16[256,256]{1,0:T(8,128)(2,1)}, u32[]{:S(2)}, u32[]{:S(2)}) collective-permute-start(bf16[256,256]{1,0:T(8,128)(2,1)S(1)} %convolution_convert_fusion.2), channel_id=1, source_target_pairs={{0,1},{1,2},{2,3},{3,4},{4,5},{5,6},{6,7},{7,8},{8,9},{9,10},{10,1... | collective-permute-start | bytes 393224 | tf_op jit(solution)/shard_map/ppermute | solution.py:14
  10.8 40.4 %collective-permute-start.6 = (bf16[256,256]{1,0:T(8,128)(2,1)S(1)}, bf16[256,256]{1,0:T(8,128)(2,1)}, u32[]{:S(2)}, u32[]{:S(2)}) collective-permute-start(bf16[256,256]{1,0:T(8,128)(2,1)S(1)} %convolution_convert_fusion.2), channel_id=1, source_target_pairs={{0,2},{1,3},{2,4},{3,5},{4,6},{5,7},{6,8},{7,9},{8,10},{9,11},{10,... | collective-permute-start | bytes 393224 | tf_op jit(solution)/shard_map/ppermute | solution.py:14
  14.0 36.3 %collective-permute-start.5 = (bf16[256,256]{1,0:T(8,128)(2,1)S(1)}, bf16[256,256]{1,0:T(8,128)(2,1)}, u32[]{:S(2)}, u32[]{:S(2)}) collective-permute-start(bf16[256,256]{1,0:T(8,128)(2,1)S(1)} %convolution_convert_fusion.2), channel_id=1, source_target_pairs={{0,3},{1,4},{2,5},{3,6},{4,7},{5,8},{6,9},{7,10},{8,11},{9,12},{10... | collective-permute-start | bytes 393224 | tf_op jit(solution)/shard_map/ppermute | solution.py:14
  19.6 17.8 %collective-permute-start.1 = (bf16[256,256]{1,0:T(8,128)(2,1)S(1)}, bf16[256,256]{1,0:T(8,128)(2,1)}, u32[]{:S(2)}, u32[]{:S(2)}) collective-permute-start(bf16[256,256]{1,0:T(8,128)(2,1)S(1)} %convolution_convert_fusion.3), channel_id=1, source_target_pairs={{0,3},{1,4},{2,5},{3,6},{4,7},{5,8},{6,9},{7,10},{8,11},{9,12},{10... | collective-permute-start | bytes 393224 | tf_op jit(solution)/shard_map/ppermute | solution.py:14
  22.8 9.3 %collective-permute-start = (bf16[256,256]{1,0:T(8,128)(2,1)S(1)}, bf16[256,256]{1,0:T(8,128)(2,1)S(1)}, u32[]{:S(2)}, u32[]{:S(2)}) collective-permute-start(bf16[256,256]{1,0:T(8,128)(2,1)S(1)} %convolution_convert_fusion.3), channel_id=1, source_target_pairs={{0,4},{1,5},{2,6},{3,7},{4,8},{5,9},{6,10},{7,11},{8,12},{9,13},{1... | collective-permute-start | bytes 393224 | tf_op jit(solution)/shard_map/ppermute | solution.py:14
  26.6 4.1 copy-start.6
  32.8 8.2 %collective-permute-start.2 = (bf16[256,256]{1,0:T(8,128)(2,1)S(1)}, bf16[256,256]{1,0:T(8,128)(2,1)S(1)}, u32[]{:S(2)}, u32[]{:S(2)}) collective-permute-start(bf16[256,256]{1,0:T(8,128)(2,1)S(1)} %convolution_convert_fusion.3), channel_id=1, source_target_pairs={{0,2},{1,3},{2,4},{3,5},{4,6},{5,7},{6,8},{7,9},{8,10},{9,11},{10,... | collective-permute-start | bytes 393224 | tf_op jit(solution)/shard_map/ppermute | solution.py:14
  37.4 9.7 %collective-permute-start.3 = (bf16[256,256]{1,0:T(8,128)(2,1)S(1)}, bf16[256,256]{1,0:T(8,128)(2,1)S(1)}, u32[]{:S(2)}, u32[]{:S(2)}) collective-permute-start(bf16[256,256]{1,0:T(8,128)(2,1)S(1)} %convolution_convert_fusion.3), channel_id=1, source_target_pairs={{0,1},{1,2},{2,3},{3,4},{4,5},{5,6},{6,7},{7,8},{8,9},{9,10},{10,1... | collective-permute-start | bytes 393224 | tf_op jit(solution)/shard_map/ppermute | solution.py:14
  41.0 9.3 %collective-permute-start.4 = (bf16[256,256]{1,0:T(8,128)(2,1)S(1)}, bf16[256,256]{1,0:T(8,128)(2,1)S(1)}, u32[]{:S(2)}, u32[]{:S(2)}) collective-permute-start(bf16[256,256]{1,0:T(8,128)(2,1)S(1)} %convolution_convert_fusion.2), channel_id=1, source_target_pairs={{0,4},{1,5},{2,6},{3,7},{4,8},{5,9},{6,10},{7,11},{8,12},{9,13},{1... | collective-permute-start | bytes 393224 | tf_op jit(solution)/shard_map/ppermute | solution.py:14
  47.1 6.9 %copy-start.10 = (pred[1280]{0:T(1024)(128)(4,1)S(1)}, pred[1280]{0:T(1024)(128)(4,1)}, u32[]{:S(2)}) copy-start(pred[1280]{0:T(1024)(128)(4,1)} %broadcast_compare_fusion) | copy-start | bytes 3844
  47.1 6.8 %copy-start.11 = (s32[1,256]{1,0:T(1,128)S(1)}, s32[1,256]{1,0:T(1,128)}, u32[]{:S(2)}) copy-start(s32[1,256]{1,0:T(1,128)} %constant_dynamic-slice_fusion) | copy-start | bytes 3076
  47.1 6.8 %copy-start.12 = (s32[256]{0:T(256)S(1)}, s32[256]{0:T(256)}, u32[]{:S(2)}) copy-start(s32[256]{0:T(256)} %iota_add_fusion.1) | copy-start | bytes 3076
  179.8 19.9 %collective-permute-start.12 = (f32[256,256]{0,1:T(8,128)}, f32[256,256]{0,1:T(8,128)}, u32[]{:S(2)}, u32[]{:S(2)}) collective-permute-start(f32[256,256]{0,1:T(8,128)} %bitcast.16), channel_id=1, source_target_pairs={{1,0},{2,1},{3,2},{4,3},{5,4},{6,5},{7,6},{8,7},{9,8},{10,9},{11,1... | collective-permute-start | bytes 786440 | tf_op jit(solution)/shard_map/ppermute | solution.py:14
  181.7 20.0 %collective-permute-start.13 = (f32[256,256]{0,1:T(8,128)}, f32[256,256]{0,1:T(8,128)}, u32[]{:S(2)}, u32[]{:S(2)}) collective-permute-start(f32[256,256]{0,1:T(8,128)} %bitcast.101), channel_id=1, source_target_pairs={{2,0},{3,1},{4,2},{5,3},{6,4},{7,5},{8,6},{9,7},{10,8},{11,9},{12,... | collective-permute-start | bytes 786440 | tf_op jit(solution)/shard_map/ppermute | solution.py:14
  184.0 19.7 %collective-permute-start.14 = (f32[256,256]{0,1:T(8,128)}, f32[256,256]{0,1:T(8,128)}, u32[]{:S(2)}, u32[]{:S(2)}) collective-permute-start(f32[256,256]{0,1:T(8,128)} %bitcast.98), channel_id=1, source_target_pairs={{3,0},{4,1},{5,2},{6,3},{7,4},{8,5},{9,6},{10,7},{11,8},{12,9},{13... | collective-permute-start | bytes 786440 | tf_op jit(solution)/shard_map/ppermute | solution.py:14
  185.9 27.2 %collective-permute-start.15 = (f32[256,256]{0,1:T(8,128)}, f32[256,256]{0,1:T(8,128)}, u32[]{:S(2)}, u32[]{:S(2)}) collective-permute-start(f32[256,256]{0,1:T(8,128)} %bitcast.96), channel_id=1, source_target_pairs={{4,0},{5,1},{6,2},{7,3},{8,4},{9,5},{10,6},{11,7},{12,8},{13,9},{1... | collective-permute-start | bytes 786440 | tf_op jit(solution)/shard_map/ppermute | solution.py:14
  197.8 16.6 %collective-permute-start.8 = (f32[256,256]{0,1:T(8,128)}, f32[256,256]{0,1:T(8,128)}, u32[]{:S(2)}, u32[]{:S(2)}) collective-permute-start(f32[256,256]{0,1:T(8,128)} %bitcast.102), channel_id=1, source_target_pairs={{1,0},{2,1},{3,2},{4,3},{5,4},{6,5},{7,6},{8,7},{9,8},{10,9},{11,1... | collective-permute-start | bytes 786440 | tf_op jit(solution)/shard_map/ppermute | solution.py:14
  199.8 17.0 %collective-permute-start.9 = (f32[256,256]{0,1:T(8,128)}, f32[256,256]{0,1:T(8,128)}, u32[]{:S(2)}, u32[]{:S(2)}) collective-permute-start(f32[256,256]{0,1:T(8,128)} %bitcast.100), channel_id=1, source_target_pairs={{2,0},{3,1},{4,2},{5,3},{6,4},{7,5},{8,6},{9,7},{10,8},{11,9},{12,... | collective-permute-start | bytes 786440 | tf_op jit(solution)/shard_map/ppermute | solution.py:14
  201.7 15.1 %collective-permute-start.10 = (f32[256,256]{0,1:T(8,128)}, f32[256,256]{0,1:T(8,128)}, u32[]{:S(2)}, u32[]{:S(2)}) collective-permute-start(f32[256,256]{0,1:T(8,128)} %bitcast.99), channel_id=1, source_target_pairs={{3,0},{4,1},{5,2},{6,3},{7,4},{8,5},{9,6},{10,7},{11,8},{12,9},{13... | collective-permute-start | bytes 786440 | tf_op jit(solution)/shard_map/ppermute | solution.py:14
  203.6 35.8 %collective-permute-start.11 = (f32[256,256]{0,1:T(8,128)}, f32[256,256]{0,1:T(8,128)}, u32[]{:S(2)}, u32[]{:S(2)}) collective-permute-start(f32[256,256]{0,1:T(8,128)} %bitcast.97), channel_id=1, source_target_pairs={{4,0},{5,1},{6,2},{7,3},{8,4},{9,5},{10,6},{11,7},{12,8},{13,9},{1... | collective-permute-start | bytes 786440 | tf_op jit(solution)/shard_map/ppermute | solution.py:14
  205.9 34.8 %copy-start.4 = (bf16[8,256,128]{1,2,0:T(8,128)(2,1)S(1)}, bf16[8,256,128]{1,2,0:T(8,128)(2,1)}, u32[]{:S(2)}) copy-start(bf16[8,256,128]{1,2,0:T(8,128)(2,1)} %get-tuple-element.132) | copy-start | bytes 1572868
  (13 other events, 13.4 us)
Sparse Core Ops, SparseCore 0:
  248.2 105.2 reduce-scatter.3
where the time goes:
time: 434 us; the launch traced here: 430 us
  waiting for transfers between devices  137 us (32%)
  matrix products  86.7 us (20%)
  blocking collectives  66.4 us (15%)
  starting transfers between devices  43.6 us (10%)
  local copies, waits for them, and re-layouts  42.5 us (10%)
  loops' own time  26.3 us (6%)
  between operations  14.5 us (3%)
  other arithmetic  13 us (3%)
    unnamed x2, waiting for transfers between devices  101 us
    psum x1, blocking collectives, body(): summed = lax.psum(summed, 'dp')  66.4 us
    ppermute x16, starting transfers between devices, shifted(): return lax.ppermute(block, axis, route)  43.6 us
    ppermute x16, waiting for transfers between devices, shifted(): return lax.ppermute(block, axis, route)  36 us
    another operation x1, loops' own time, body(): lax.map(lambda head_index: head_terms(head_index, queries, k_block, v_blo...  26.3 us
    dot_general x8, matrix products, head_terms(): jnp.dot(weights_b.T, dout, preferred_element_type=jnp.float32)  17.7 us
    unnamed x38, local copies, waits for them, and re-layouts  17.1 us
    dot_general x8, matrix products, head_terms(): key_gradient = jnp.dot(dscores.T, query, preferred_element_type=jnp.float32)  16.6 us
  transfers between devices with their start and end apart: 17, of which 6 were waited for; matrix products, arithmetic and copies ran while one was open for 6% of the time, Pallas kernels for 0%

commit v1 on v0

--- a/solution.py
+++ b/solution.py
@@ -119,7 +119,7 @@
         scatter_dimension=0,
         tiled=True,
     ).astype(jnp.float32)
-    summed = lax.psum(summed, "dp")
+    summed = jnp.sum(lax.all_gather(summed, "dp"), axis=0)
     norm_factor = (lax.axis_size("dp") * lax.axis_size("ctx") * rows) ** (-0.5)
     summed = summed * norm_factor
     grad_query = summed[:, :q_cols]

time: 434 us -> 445 us (1.025)
  the two profiles are of different devices: /device:TPU:16 before, /device:TPU:2 now
where the time goes in v1:
time: 445 us; the launch traced here: 441 us
  waiting for transfers between devices  216 us (49%)
  matrix products  86.8 us (20%)
  starting transfers between devices  41.3 us (9%)
  local copies, waits for them, and re-layouts  39.4 us (9%)
  loops' own time  26.3 us (6%)
  other arithmetic  16.7 us (4%)
  between operations  14.4 us (3%)
    reduce_scatter x1, waiting for transfers between devices, body(): lax.psum_scatter(lax.optimization_barrier(partial_value.astype(jnp.bfloat...  107 us
    all_gather x1, waiting for transfers between devices, body(): summed = jnp.sum(lax.all_gather(summed, 'dp'), axis=0)  72.4 us
    ppermute x16, starting transfers between devices, shifted(): return lax.ppermute(block, axis, route)  41.2 us
    ppermute x16, waiting for transfers between devices, shifted(): return lax.ppermute(block, axis, route)  36.6 us
    another operation x1, loops' own time, body(): lax.map(lambda head_index: head_terms(head_index, queries, k_block, v_blo...  26.3 us
    dot_general x8, matrix products, head_terms(): jnp.dot(weights_b.T, dout, preferred_element_type=jnp.float32)  17.8 us
    dot_general x8, matrix products, head_terms(): key_gradient = jnp.dot(dscores.T, query, preferred_element_type=jnp.float32)  16.5 us
    slice x12, local copies, waits for them, and re-layouts, piece(): return (dk_local[first:first + rows], dv_local[first:first + rows])  13.5 us
  transfers between devices with their start and end apart: 18, of which 10 were waited for; matrix products, arithmetic and copies ran while one was open for 6% of the time, Pallas kernels for 0%

profile of v1, /device:TPU:2, one launch (start us, length us, event | category | flops | bytes accessed | tf_op | source)
XLA Modules:
  0.0 441.2 jit_solution(299095003918343910)
XLA Ops:
  10.8 3.5 collective-permute-start.6
  14.3 4.2 collective-permute-start.5
  20.0 2.8 collective-permute-start.1
  22.8 5.1 %collective-permute-start = (bf16[256,256]{1,0:T(8,128)(2,1)S(1)}, bf16[256,256]{1,0:T(8,128)(2,1)S(1)}, u32[]{:S(2)}, u32[]{:S(2)}) collective-permute-start(bf16[256,256]{1,0:T(8,128)(2,1)S(1)} %convolution_convert_fusion.3), channel_id=1, source_target_pairs={{0,4},{1,5},{2,6},{3,7},{4,8},{5,9},{6,10},{7,11},{8,12},{9,13},{1... | collective-permute-start | bytes 393224 | tf_op jit(solution)/shard_map/ppermute | solution.py:14
  34.2 3.2 collective-permute-start.2
  41.2 2.7 collective-permute-done.2
  43.9 2.3 collective-permute-start.4
  46.8 6.3 %collective-permute-done.4 = bf16[256,256]{1,0:T(8,128)(2,1)S(1)} collective-permute-done((bf16[256,256]{1,0:T(8,128)(2,1)S(1)}, bf16[256,256]{1,0:T(8,128)(2,1)S(1)}, u32[]{:S(2)}, u32[]{:S(2)}) %collective-permute-start.4) | collective-permute-done | bytes 131104 | tf_op jit(solution)/shard_map/ppermute | solution.py:14
  56.8 116.8 %while.17 = (s32[]{:T(128)}, bf16[8,256,128]{1,2,0:T(8,128)(2,1)}, f32[8,1280,128]{2,1,0:T(8,128)}, f32[8,1280,128]{2,1,0:T(8,128)}, s32[8]{0:T(128)S(1)}, /*ind...) while((s32[]{:T(128)}, bf16[8,256,128]{1,2,0:T(8,128)(2,1)}, ...), condition=%wide.region_4.5_spmd.clone, body=%wide.region_0.4_spmd.clone.sunk | while | flops 511278368 | bytes 14253591 | solution.py:74
  67.1 2.2 fusion.103
  125.4 2.3 fusion.103
  140.1 2.3 fusion.103
  169.3 2.2 fusion.103
  173.6 2.9 bitcast_reduce_fusion
  182.6 2.6 collective-permute-start.12
  191.3 2.9 bitcast_reduce_fusion.1
  212.7 10.6 %collective-permute-done.8 = f32[256,256]{0,1:T(8,128)} collective-permute-done((f32[256,256]{0,1:T(8,128)}, f32[256,256]{0,1:T(8,128)}, u32[]{:S(2)}, u32[]{:S(2)}) %collective-permute-start.8) | collective-permute-done | bytes 262176 | tf_op jit(solution)/shard_map/ppermute | solution.py:14
  223.2 7.1 %collective-permute-done.9 = f32[256,256]{0,1:T(8,128)} collective-permute-done((f32[256,256]{0,1:T(8,128)}, f32[256,256]{0,1:T(8,128)}, u32[]{:S(2)}, u32[]{:S(2)}) %collective-permute-start.9) | collective-permute-done | bytes 262176 | tf_op jit(solution)/shard_map/ppermute | solution.py:14
  230.4 4.5 %collective-permute-done.10 = f32[256,256]{0,1:T(8,128)} collective-permute-done((f32[256,256]{0,1:T(8,128)}, f32[256,256]{0,1:T(8,128)}, u32[]{:S(2)}, u32[]{:S(2)}) %collective-permute-start.10) | collective-permute-done | bytes 262176 | tf_op jit(solution)/shard_map/ppermute | solution.py:14
  234.9 2.8 collective-permute-done.11
  239.0 2.7 fusion.33
  241.7 4.6 %copy.43 = bf16[1024,1536]{1,0:T(8,128)(2,1)} copy(bf16[1024,1536]{0,1:T(8,128)(2,1)} %fusion.33) | data formatting | bytes 6291456
  246.4 107.3 %reduce-scatter.4.cloned.1.call-done = bf16[32,1536]{1,0:T(8,128)(2,1)} async-done(((bf16[1024,1536]{1,0:T(8,128)(2,1)}), bf16[32,1536]{1,0:T(8,128)(2,1)}) %reduce-scatter.4.cloned.1.call-update) | async-done | bytes 98320 | tf_op jit(solution)/shard_map/reduce_scatter | solution.py:114
  358.5 72.4 %all-gather.3.cloned.1.call-done = f32[512,1536]{1,0:T(8,128)} async-done(((f32[32,1536]{1,0:T(8,128)}), f32[512,1536]{1,0:T(8,128)}) %all-gather.3.cloned.1.call-update) | async-done | bytes 3145744 | tf_op jit(solution)/shard_map/all_gather | solution.py:122
  (167 shorter events, 141.1 us)
Async XLA Ops:
  7.2 21.4 %copy-start = (bf16[1024,1024]{1,0:T(8,128)(2,1)S(1)}, bf16[1024,1024]{1,0:T(8,128)(2,1)}, u32[]{:S(2)}) copy-start(bf16[1024,1024]{1,0:T(8,128)(2,1)} %param.9) | copy-start | bytes 6291460
  7.2 21.3 %copy-start.2 = (bf16[1,256,1024]{2,1,0:T(8,128)(2,1)S(1)}, bf16[1,256,1024]{2,1,0:T(8,128)(2,1)}, u32[]{:S(2)}) copy-start(bf16[1,256,1024]{2,1,0:T(8,128)(2,1)} %param.8) | copy-start | bytes 1572868
  7.2 346.5 %reduce-scatter.4.cloned.1.call-start = ((), (), s32[]{:S(2)}) async-start(), calls=%async_computation.2 | async-start | bytes 3244032 | tf_op jit(solution)/shard_map/reduce_scatter | solution.py:114
  8.9 46.1 %collective-permute-start.7 = (bf16[256,256]{1,0:T(8,128)(2,1)S(1)}, bf16[256,256]{1,0:T(8,128)(2,1)}, u32[]{:S(2)}, u32[]{:S(2)}) collective-permute-start(bf16[256,256]{1,0:T(8,128)(2,1)S(1)} %convolution_convert_fusion.2), channel_id=1, source_target_pairs={{0,1},{1,2},{2,3},{3,4},{4,5},{5,6},{6,7},{7,8},{8,9},{9,10},{10,1... | collective-permute-start | bytes 393224 | tf_op jit(solution)/shard_map/ppermute | solution.py:14
  10.8 43.2 %collective-permute-start.6 = (bf16[256,256]{1,0:T(8,128)(2,1)S(1)}, bf16[256,256]{1,0:T(8,128)(2,1)}, u32[]{:S(2)}, u32[]{:S(2)}) collective-permute-start(bf16[256,256]{1,0:T(8,128)(2,1)S(1)} %convolution_convert_fusion.2), channel_id=1, source_target_pairs={{0,2},{1,3},{2,4},{3,5},{4,6},{5,7},{6,8},{7,9},{8,10},{9,11},{10,... | collective-permute-start | bytes 393224 | tf_op jit(solution)/shard_map/ppermute | solution.py:14
  14.3 38.8 %collective-permute-start.5 = (bf16[256,256]{1,0:T(8,128)(2,1)S(1)}, bf16[256,256]{1,0:T(8,128)(2,1)}, u32[]{:S(2)}, u32[]{:S(2)}) collective-permute-start(bf16[256,256]{1,0:T(8,128)(2,1)S(1)} %convolution_convert_fusion.2), channel_id=1, source_target_pairs={{0,3},{1,4},{2,5},{3,6},{4,7},{5,8},{6,9},{7,10},{8,11},{9,12},{10... | collective-permute-start | bytes 393224 | tf_op jit(solution)/shard_map/ppermute | solution.py:14
  20.0 18.3 %collective-permute-start.1 = (bf16[256,256]{1,0:T(8,128)(2,1)S(1)}, bf16[256,256]{1,0:T(8,128)(2,1)}, u32[]{:S(2)}, u32[]{:S(2)}) collective-permute-start(bf16[256,256]{1,0:T(8,128)(2,1)S(1)} %convolution_convert_fusion.3), channel_id=1, source_target_pairs={{0,3},{1,4},{2,5},{3,6},{4,7},{5,8},{6,9},{7,10},{8,11},{9,12},{10... | collective-permute-start | bytes 393224 | tf_op jit(solution)/shard_map/ppermute | solution.py:14
  22.8 10.8 %collective-permute-start = (bf16[256,256]{1,0:T(8,128)(2,1)S(1)}, bf16[256,256]{1,0:T(8,128)(2,1)S(1)}, u32[]{:S(2)}, u32[]{:S(2)}) collective-permute-start(bf16[256,256]{1,0:T(8,128)(2,1)S(1)} %convolution_convert_fusion.3), channel_id=1, source_target_pairs={{0,4},{1,5},{2,6},{3,7},{4,8},{5,9},{6,10},{7,11},{8,12},{9,13},{1... | collective-permute-start | bytes 393224 | tf_op jit(solution)/shard_map/ppermute | solution.py:14
  34.2 9.6 %collective-permute-start.2 = (bf16[256,256]{1,0:T(8,128)(2,1)S(1)}, bf16[256,256]{1,0:T(8,128)(2,1)S(1)}, u32[]{:S(2)}, u32[]{:S(2)}) collective-permute-start(bf16[256,256]{1,0:T(8,128)(2,1)S(1)} %convolution_convert_fusion.3), channel_id=1, source_target_pairs={{0,2},{1,3},{2,4},{3,5},{4,6},{5,7},{6,8},{7,9},{8,10},{9,11},{10,... | collective-permute-start | bytes 393224 | tf_op jit(solution)/shard_map/ppermute | solution.py:14
  38.4 8.4 %collective-permute-start.3 = (bf16[256,256]{1,0:T(8,128)(2,1)S(1)}, bf16[256,256]{1,0:T(8,128)(2,1)S(1)}, u32[]{:S(2)}, u32[]{:S(2)}) collective-permute-start(bf16[256,256]{1,0:T(8,128)(2,1)S(1)} %convolution_convert_fusion.3), channel_id=1, source_target_pairs={{0,1},{1,2},{2,3},{3,4},{4,5},{5,6},{6,7},{7,8},{8,9},{9,10},{10,1... | collective-permute-start | bytes 393224 | tf_op jit(solution)/shard_map/ppermute | solution.py:14
  43.9 9.3 %collective-permute-start.4 = (bf16[256,256]{1,0:T(8,128)(2,1)S(1)}, bf16[256,256]{1,0:T(8,128)(2,1)S(1)}, u32[]{:S(2)}, u32[]{:S(2)}) collective-permute-start(bf16[256,256]{1,0:T(8,128)(2,1)S(1)} %convolution_convert_fusion.2), channel_id=1, source_target_pairs={{0,4},{1,5},{2,6},{3,7},{4,8},{5,9},{6,10},{7,11},{8,12},{9,13},{1... | collective-permute-start | bytes 393224 | tf_op jit(solution)/shard_map/ppermute | solution.py:14
  46.8 10.0 %copy-start.10 = (pred[1280]{0:T(1024)(128)(4,1)S(1)}, pred[1280]{0:T(1024)(128)(4,1)}, u32[]{:S(2)}) copy-start(pred[1280]{0:T(1024)(128)(4,1)} %broadcast_compare_fusion) | copy-start | bytes 3844
  46.8 10.0 %copy-start.11 = (s32[1,256]{1,0:T(1,128)S(1)}, s32[1,256]{1,0:T(1,128)}, u32[]{:S(2)}) copy-start(s32[1,256]{1,0:T(1,128)} %constant_dynamic-slice_fusion) | copy-start | bytes 3076
  182.6 20.7 %collective-permute-start.12 = (f32[256,256]{0,1:T(8,128)}, f32[256,256]{0,1:T(8,128)}, u32[]{:S(2)}, u32[]{:S(2)}) collective-permute-start(f32[256,256]{0,1:T(8,128)} %bitcast.16), channel_id=1, source_target_pairs={{1,0},{2,1},{3,2},{4,3},{5,4},{6,5},{7,6},{8,7},{9,8},{10,9},{11,1... | collective-permute-start | bytes 786440 | tf_op jit(solution)/shard_map/ppermute | solution.py:14
  185.2 20.0 %collective-permute-start.13 = (f32[256,256]{0,1:T(8,128)}, f32[256,256]{0,1:T(8,128)}, u32[]{:S(2)}, u32[]{:S(2)}) collective-permute-start(f32[256,256]{0,1:T(8,128)} %bitcast.103), channel_id=1, source_target_pairs={{2,0},{3,1},{4,2},{5,3},{6,4},{7,5},{8,6},{9,7},{10,8},{11,9},{12,... | collective-permute-start | bytes 786440 | tf_op jit(solution)/shard_map/ppermute | solution.py:14
  187.4 19.8 %collective-permute-start.14 = (f32[256,256]{0,1:T(8,128)}, f32[256,256]{0,1:T(8,128)}, u32[]{:S(2)}, u32[]{:S(2)}) collective-permute-start(f32[256,256]{0,1:T(8,128)} %bitcast.100), channel_id=1, source_target_pairs={{3,0},{4,1},{5,2},{6,3},{7,4},{8,5},{9,6},{10,7},{11,8},{12,9},{13... | collective-permute-start | bytes 786440 | tf_op jit(solution)/shard_map/ppermute | solution.py:14
  189.3 22.1 %collective-permute-start.15 = (f32[256,256]{0,1:T(8,128)}, f32[256,256]{0,1:T(8,128)}, u32[]{:S(2)}, u32[]{:S(2)}) collective-permute-start(f32[256,256]{0,1:T(8,128)} %bitcast.98), channel_id=1, source_target_pairs={{4,0},{5,1},{6,2},{7,3},{8,4},{9,5},{10,6},{11,7},{12,8},{13,9},{1... | collective-permute-start | bytes 786440 | tf_op jit(solution)/shard_map/ppermute | solution.py:14
  201.3 22.0 %collective-permute-start.8 = (f32[256,256]{0,1:T(8,128)}, f32[256,256]{0,1:T(8,128)}, u32[]{:S(2)}, u32[]{:S(2)}) collective-permute-start(f32[256,256]{0,1:T(8,128)} %bitcast.104), channel_id=1, source_target_pairs={{1,0},{2,1},{3,2},{4,3},{5,4},{6,5},{7,6},{8,7},{9,8},{10,9},{11,1... | collective-permute-start | bytes 786440 | tf_op jit(solution)/shard_map/ppermute | solution.py:14
  203.3 27.1 %collective-permute-start.9 = (f32[256,256]{0,1:T(8,128)}, f32[256,256]{0,1:T(8,128)}, u32[]{:S(2)}, u32[]{:S(2)}) collective-permute-start(f32[256,256]{0,1:T(8,128)} %bitcast.102), channel_id=1, source_target_pairs={{2,0},{3,1},{4,2},{5,3},{6,4},{7,5},{8,6},{9,7},{10,8},{11,9},{12,... | collective-permute-start | bytes 786440 | tf_op jit(solution)/shard_map/ppermute | solution.py:14
  205.2 29.7 %collective-permute-start.10 = (f32[256,256]{0,1:T(8,128)}, f32[256,256]{0,1:T(8,128)}, u32[]{:S(2)}, u32[]{:S(2)}) collective-permute-start(f32[256,256]{0,1:T(8,128)} %bitcast.101), channel_id=1, source_target_pairs={{3,0},{4,1},{5,2},{6,3},{7,4},{8,5},{9,6},{10,7},{11,8},{12,9},{13... | collective-permute-start | bytes 786440 | tf_op jit(solution)/shard_map/ppermute | solution.py:14
  207.2 30.5 %collective-permute-start.11 = (f32[256,256]{0,1:T(8,128)}, f32[256,256]{0,1:T(8,128)}, u32[]{:S(2)}, u32[]{:S(2)}) collective-permute-start(f32[256,256]{0,1:T(8,128)} %bitcast.99), channel_id=1, source_target_pairs={{4,0},{5,1},{6,2},{7,3},{8,4},{9,5},{10,6},{11,7},{12,8},{13,9},{1... | collective-permute-start | bytes 786440 | tf_op jit(solution)/shard_map/ppermute | solution.py:14
  209.4 29.6 %copy-start.4 = (bf16[8,256,128]{1,2,0:T(8,128)(2,1)S(1)}, bf16[8,256,128]{1,2,0:T(8,128)(2,1)}, u32[]{:S(2)}) copy-start(bf16[8,256,128]{1,2,0:T(8,128)(2,1)} %get-tuple-element.132) | copy-start | bytes 1572868
  246.3 109.0 %copy-start.5 = (bf16[8,256,128]{1,2,0:T(8,128)(2,1)S(1)}, bf16[8,256,128]{1,2,0:T(8,128)(2,1)}, u32[]{:S(2)}) copy-start(bf16[8,256,128]{1,2,0:T(8,128)(2,1)} %get-tuple-element.132) | copy-start | bytes 1572868
  246.3 184.6 %all-gather.3.cloned.1.call-start = ((), (), s32[]{:S(2)}) async-start(), calls=%async_computation.1 | async-start | bytes 3342336 | tf_op jit(solution)/shard_map/all_gather | solution.py:122
  (14 other events, 26.4 us)
Sparse Core Ops, SparseCore 0:
  246.5 107.1 reduce-scatter.3
  355.7 75.1 all-gather.2
